TPU v7x, 32 devices: a whole 2x2x4 slice. The times are simulated.
32 devices in a mesh: rows: 8 (over z, y), cols: 4 (over x, core).
Axes of the slice: x: 2, y: 2, z: 4, core: 2. Of those that a mesh axis runs over, the one named last changes fastest.
Arguments:
- start_panel: float32 [64, 16384], P(None, ('rows', 'cols')), may hold values from -6 to 6
- tile_values: float32 [128, 16, 128, 128], P('rows', 'cols')
- tile_column: int32 [128, 16], P('rows', 'cols'), may hold values from 0 to 127, as said below
- tile_count: int32 [128], P('rows'), may hold values from 8 to 16, as said below
Outputs:
- basis: float32 [64, 16384], P(None, ('rows', 'cols'))
Inputs may be any that keep to these rules, and one draw needn't show every extreme that they name: `tile_count`: every row block has between half of its slots and all 16 slots live; some row block has all 16 live. `tile_column`: in row block i the entries are distinct column blocks, each within 16 blocks of i, and the first is i itself; slots at or beyond tile_count[i] hold such entries too but are not used.
All inputs are finite; a program needn't handle non-finite values.
Results may differ from a plain program's by a relative error of at most 0.0003.
Values sent between devices are 32-bit elements; how exact they have to be, the bound alone decides.
A program may use at most 64 MiB of HBM per device.

v0:
```python
import math
import jax
import jax.numpy as jnp
from jax import lax
from jax.sharding import PartitionSpec as P

ITERS = 3


def with_halo(block, sides, width):
    for axis, dim in sides:
        count = lax.axis_size(axis)
        forward = [(i, i + 1) for i in range(count - 1)]
        backward = [(target, source) for source, target in forward]
        low = lax.ppermute(
            lax.slice_in_dim(block, block.shape[dim] - width, None, axis=dim), axis, forward
        )
        high = lax.ppermute(lax.slice_in_dim(block, 0, width, axis=dim), axis, backward)
        block = jnp.concatenate([low, block, high], axis=dim)
    return block


def local_product(extended, tile_values, tile_column, tile_count):
    owned_blocks = tile_values.shape[0]
    slot_dev = tile_values.shape[1]
    tile_width = tile_values.shape[2]
    anchor = lax.axis_index("rows") * owned_blocks - owned_blocks
    local_column = tile_column - anchor
    blocks = extended.reshape(extended.shape[0], 3 * owned_blocks, tile_width)
    picked = jnp.take(blocks, local_column, axis=1)
    slot_ids = lax.axis_index("cols") * slot_dev + jnp.arange(slot_dev, dtype=jnp.int32)
    alive_mask = slot_ids[None, :] < tile_count[:, None]
    picked = jnp.where(alive_mask[None, :, :, None], picked, jnp.float32(0.0))
    result = jnp.einsum("disk,isnk->din", picked, tile_values, precision=lax.Precision.HIGHEST)
    return result.reshape(extended.shape[0], owned_blocks * tile_width)


def per_device(start_panel, tile_values, tile_column, tile_count):

    def fetch_owner(panel_part):
        return lax.all_gather(panel_part, "cols", axis=1, tiled=True)

    def partial_of(owner_panel):
        extended = with_halo(owner_panel, (("rows", 1),), owner_panel.shape[1])
        return local_product(extended, tile_values, tile_column, tile_count)

    def reduce_share(partial_terms):
        return lax.psum_scatter(partial_terms, "cols", scatter_dimension=1, tiled=True)

    panel = start_panel
    for sweep_index in range(ITERS):
        first_terms = partial_of(fetch_owner(panel))
        middle = fetch_owner(reduce_share(first_terms))
        second = reduce_share(partial_of(middle))
        local_gram = jnp.dot(
            second, second.T, precision=lax.Precision.HIGHEST, preferred_element_type=jnp.float32
        )
        lower_factor = jnp.linalg.cholesky(lax.psum(local_gram, ("rows", "cols")))
        panel = lax.linalg.triangular_solve(lower_factor, second, left_side=True, lower=True)
    scaling = math.sqrt(lax.axis_size("rows") * lax.axis_size("cols") * panel.shape[1])
    return panel * jnp.float32(scaling)


def solution(mesh):
    in_specs = (
        P(None, ("rows", "cols")),
        P("rows", "cols", None, None),
        P("rows", "cols"),
        P("rows"),
    )
    out_specs = P(None, ("rows", "cols"))
    return jax.shard_map(
        per_device, mesh=mesh, in_specs=in_specs, out_specs=out_specs, check_vma=False
    )
```

profile of v0, /device:TPU:0, one launch (start us, length us, event | category | flops | bytes accessed | tf_op | source)
XLA Modules:
  0.0 582.8 jit_solution(2102967249004942591)
XLA Ops:
  6.5 8.8 %all_gather.18 = f32[64,2048]{1,0:T(8,128)S(1)} all-gather(f32[64,512]{1,0:T(8,128)} %param.9), channel_id=1, replica_groups=mesh['rows'=8,'cols'=4] {'cols'}, dimensions={1}, use_global_device_ids=true | all-gather | bytes 655360 | tf_op jit(solution)/shard_map/all_gather | solution.py:41
  23.0 8.5 %collective-permute-done.1 = f32[64,2048]{1,0:T(8,128)S(1)} collective-permute-done((f32[64,2048]{1,0:T(8,128)S(1)}, f32[64,2048]{1,0:T(8,128)S(1)}, u32[]{:S(2)}, u32[]{:S(2)}) %collective-permute-start.1) | collective-permute-done | bytes 524320 | tf_op jit(solution)/shard_map/ppermute | solution.py:18
  31.4 11.2 %collective-permute-done = f32[64,2048]{1,0:T(8,128)S(1)} collective-permute-done((f32[64,2048]{1,0:T(8,128)S(1)}, f32[64,2048]{1,0:T(8,128)S(1)}, u32[]{:S(2)}, u32[]{:S(2)}) %collective-permute-start) | collective-permute-done | bytes 524320 | tf_op jit(solution)/shard_map/ppermute | solution.py:15
  53.2 22.6 %reduce-scatter.7.cloned.1.call-done = f32[64,512]{1,0:T(8,128)} async-done(((f32[64,2048]{1,0:T(8,128)}), f32[64,512]{1,0:T(8,128)}) %reduce-scatter.7.cloned.1.call-update) | async-done | bytes 131088 | tf_op jit(solution)/shard_map/reduce_scatter | solution.py:48
  88.6 10.2 %collective-permute-done.3 = f32[64,2048]{1,0:T(8,128)S(1)} collective-permute-done((f32[64,2048]{1,0:T(8,128)S(1)}, f32[64,2048]{1,0:T(8,128)S(1)}, u32[]{:S(2)}, u32[]{:S(2)}) %collective-permute-start.3) | collective-permute-done | bytes 524320 | tf_op jit(solution)/shard_map/ppermute | solution.py:18
  98.8 11.1 %collective-permute-done.2 = f32[64,2048]{1,0:T(8,128)S(1)} collective-permute-done((f32[64,2048]{1,0:T(8,128)S(1)}, f32[64,2048]{1,0:T(8,128)S(1)}, u32[]{:S(2)}, u32[]{:S(2)}) %collective-permute-start.2) | collective-permute-done | bytes 524320 | tf_op jit(solution)/shard_map/ppermute | solution.py:15
  120.5 22.2 %reduce-scatter.9.cloned.1.call-done = f32[64,512]{1,0:T(8,128)} async-done(((f32[64,2048]{1,0:T(8,128)}), f32[64,512]{1,0:T(8,128)}) %reduce-scatter.9.cloned.1.call-update) | async-done | bytes 131088 | tf_op jit(solution)/shard_map/reduce_scatter | solution.py:48
  143.9 39.7 %psum.21 = f32[64,64]{0,1:T(8,128)S(1)} all-reduce(f32[64,64]{0,1:T(8,128)S(1)} %fusion.69), channel_id=1, replica_groups=mesh['rows'=8,'cols'=4] {'rows','cols'}, use_global_device_ids=true, to_apply=%region_2.4 | all-reduce | flops 4096 | bytes 32768 | tf_op jit(solution)/shard_map/psum | solution.py:58
  197.0 7.9 %all_gather.20 = f32[64,2048]{1,0:T(8,128)S(1)} all-gather(f32[64,512]{1,0:T(8,128)S(1)} %fusion.50), channel_id=1, replica_groups=mesh['rows'=8,'cols'=4] {'cols'}, dimensions={1}, use_global_device_ids=true | all-gather | bytes 655360 | tf_op jit(solution)/shard_map/all_gather | solution.py:41
  210.8 10.2 %collective-permute-done.5 = f32[64,2048]{1,0:T(8,128)S(1)} collective-permute-done((f32[64,2048]{1,0:T(8,128)S(1)}, f32[64,2048]{1,0:T(8,128)S(1)}, u32[]{:S(2)}, u32[]{:S(2)}) %collective-permute-start.5) | collective-permute-done | bytes 524320 | tf_op jit(solution)/shard_map/ppermute | solution.py:18
  221.0 11.2 %collective-permute-done.4 = f32[64,2048]{1,0:T(8,128)S(1)} collective-permute-done((f32[64,2048]{1,0:T(8,128)S(1)}, f32[64,2048]{1,0:T(8,128)S(1)}, u32[]{:S(2)}, u32[]{:S(2)}) %collective-permute-start.4) | collective-permute-done | bytes 524320 | tf_op jit(solution)/shard_map/ppermute | solution.py:15
  242.7 22.1 %reduce-scatter.11.cloned.1.call-done = f32[64,512]{1,0:T(8,128)} async-done(((f32[64,2048]{1,0:T(8,128)}), f32[64,512]{1,0:T(8,128)}) %reduce-scatter.11.cloned.1.call-update) | async-done | bytes 131088 | tf_op jit(solution)/shard_map/reduce_scatter | solution.py:48
  277.7 10.2 %collective-permute-done.7 = f32[64,2048]{1,0:T(8,128)S(1)} collective-permute-done((f32[64,2048]{1,0:T(8,128)S(1)}, f32[64,2048]{1,0:T(8,128)S(1)}, u32[]{:S(2)}, u32[]{:S(2)}) %collective-permute-start.7) | collective-permute-done | bytes 524320 | tf_op jit(solution)/shard_map/ppermute | solution.py:18
  287.9 11.1 %collective-permute-done.6 = f32[64,2048]{1,0:T(8,128)S(1)} collective-permute-done((f32[64,2048]{1,0:T(8,128)S(1)}, f32[64,2048]{1,0:T(8,128)S(1)}, u32[]{:S(2)}, u32[]{:S(2)}) %collective-permute-start.6) | collective-permute-done | bytes 524320 | tf_op jit(solution)/shard_map/ppermute | solution.py:15
  309.6 22.2 %reduce-scatter.13.cloned.1.call-done = f32[64,512]{1,0:T(8,128)} async-done(((f32[64,2048]{1,0:T(8,128)}), f32[64,512]{1,0:T(8,128)}) %reduce-scatter.13.cloned.1.call-update) | async-done | bytes 131088 | tf_op jit(solution)/shard_map/reduce_scatter | solution.py:48
  333.0 39.7 %psum.22 = f32[64,64]{0,1:T(8,128)S(1)} all-reduce(f32[64,64]{0,1:T(8,128)S(1)} %fusion.70), channel_id=1, replica_groups=mesh['rows'=8,'cols'=4] {'rows','cols'}, use_global_device_ids=true, to_apply=%region_7.11 | all-reduce | flops 4096 | bytes 32768 | tf_op jit(solution)/shard_map/psum | solution.py:58
  386.1 7.9 %all_gather.22 = f32[64,2048]{1,0:T(8,128)S(1)} all-gather(f32[64,512]{1,0:T(8,128)S(1)} %fusion.47), channel_id=1, replica_groups=mesh['rows'=8,'cols'=4] {'cols'}, dimensions={1}, use_global_device_ids=true | all-gather | bytes 655360 | tf_op jit(solution)/shard_map/all_gather | solution.py:41
  400.0 10.2 %collective-permute-done.9 = f32[64,2048]{1,0:T(8,128)S(1)} collective-permute-done((f32[64,2048]{1,0:T(8,128)S(1)}, f32[64,2048]{1,0:T(8,128)S(1)}, u32[]{:S(2)}, u32[]{:S(2)}) %collective-permute-start.9) | collective-permute-done | bytes 524320 | tf_op jit(solution)/shard_map/ppermute | solution.py:18
  410.1 11.2 %collective-permute-done.8 = f32[64,2048]{1,0:T(8,128)S(1)} collective-permute-done((f32[64,2048]{1,0:T(8,128)S(1)}, f32[64,2048]{1,0:T(8,128)S(1)}, u32[]{:S(2)}, u32[]{:S(2)}) %collective-permute-start.8) | collective-permute-done | bytes 524320 | tf_op jit(solution)/shard_map/ppermute | solution.py:15
  431.9 22.0 %reduce-scatter.15.cloned.1.call-done = f32[64,512]{1,0:T(8,128)} async-done(((f32[64,2048]{1,0:T(8,128)}), f32[64,512]{1,0:T(8,128)}) %reduce-scatter.15.cloned.1.call-update) | async-done | bytes 131088 | tf_op jit(solution)/shard_map/reduce_scatter | solution.py:48
  466.8 10.2 %collective-permute-done.11 = f32[64,2048]{1,0:T(8,128)S(1)} collective-permute-done((f32[64,2048]{1,0:T(8,128)S(1)}, f32[64,2048]{1,0:T(8,128)S(1)}, u32[]{:S(2)}, u32[]{:S(2)}) %collective-permute-start.11) | collective-permute-done | bytes 524320 | tf_op jit(solution)/shard_map/ppermute | solution.py:18
  477.0 11.1 %collective-permute-done.10 = f32[64,2048]{1,0:T(8,128)S(1)} collective-permute-done((f32[64,2048]{1,0:T(8,128)S(1)}, f32[64,2048]{1,0:T(8,128)S(1)}, u32[]{:S(2)}, u32[]{:S(2)}) %collective-permute-start.10) | collective-permute-done | bytes 524320 | tf_op jit(solution)/shard_map/ppermute | solution.py:15
  498.6 22.3 %reduce-scatter.17.cloned.1.call-done = f32[64,512]{1,0:T(8,128)} async-done(((f32[64,2048]{1,0:T(8,128)}), f32[64,512]{1,0:T(8,128)}) %reduce-scatter.17.cloned.1.call-update) | async-done | bytes 131088 | tf_op jit(solution)/shard_map/reduce_scatter | solution.py:48
  522.1 39.8 %psum.23 = f32[64,64]{0,1:T(8,128)S(1)} all-reduce(f32[64,64]{0,1:T(8,128)S(1)} %fusion.71), channel_id=1, replica_groups=mesh['rows'=8,'cols'=4] {'rows','cols'}, use_global_device_ids=true, to_apply=%region_10.14 | all-reduce | flops 4096 | bytes 32768 | tf_op jit(solution)/shard_map/psum | solution.py:58
  (85 shorter events, 165.6 us)
Async XLA Ops:
  6.5 69.2 %reduce-scatter.7.cloned.1.call-start = ((), (), s32[]{:S(2)}) async-start(), calls=%async_computation.6 | async-start | bytes 655360 | tf_op jit(solution)/shard_map/reduce_scatter | solution.py:48
  15.4 16.1 %collective-permute-start.1 = (f32[64,2048]{1,0:T(8,128)S(1)}, f32[64,2048]{1,0:T(8,128)S(1)}, u32[]{:S(2)}, u32[]{:S(2)}) collective-permute-start(f32[64,2048]{1,0:T(8,128)S(1)} %all_gather.18), channel_id=1, source_target_pairs={{4,0},{8,4},{12,8},{16,12},{20,16},{24,20},{28,24},{5,1},{9,5},{13... | collective-permute-start | bytes 1572872 | tf_op jit(solution)/shard_map/ppermute | solution.py:18
  16.6 25.9 %collective-permute-start = (f32[64,2048]{1,0:T(8,128)S(1)}, f32[64,2048]{1,0:T(8,128)S(1)}, u32[]{:S(2)}, u32[]{:S(2)}) collective-permute-start(f32[64,2048]{1,0:T(8,128)S(1)} %all_gather.18), channel_id=1, source_target_pairs={{0,4},{4,8},{8,12},{12,16},{16,20},{20,24},{24,28},{1,5},{5,9},{9,... | collective-permute-start | bytes 1572872 | tf_op jit(solution)/shard_map/ppermute | solution.py:15
  53.1 89.5 %reduce-scatter.9.cloned.1.call-start = ((), (), s32[]{:S(2)}) async-start(), calls=%async_computation.7 | async-start | bytes 655360 | tf_op jit(solution)/shard_map/reduce_scatter | solution.py:48
  82.7 16.1 %collective-permute-start.3 = (f32[64,2048]{1,0:T(8,128)S(1)}, f32[64,2048]{1,0:T(8,128)S(1)}, u32[]{:S(2)}, u32[]{:S(2)}) collective-permute-start(f32[64,2048]{1,0:T(8,128)S(1)} %all_gather.19), channel_id=1, source_target_pairs={{4,0},{8,4},{12,8},{16,12},{20,16},{24,20},{28,24},{5,1},{9,5},{13... | collective-permute-start | bytes 1572872 | tf_op jit(solution)/shard_map/ppermute | solution.py:18
  84.0 25.9 %collective-permute-start.2 = (f32[64,2048]{1,0:T(8,128)S(1)}, f32[64,2048]{1,0:T(8,128)S(1)}, u32[]{:S(2)}, u32[]{:S(2)}) collective-permute-start(f32[64,2048]{1,0:T(8,128)S(1)} %all_gather.19), channel_id=1, source_target_pairs={{0,4},{4,8},{8,12},{12,16},{16,20},{20,24},{24,28},{1,5},{5,9},{9,... | collective-permute-start | bytes 1572872 | tf_op jit(solution)/shard_map/ppermute | solution.py:15
  120.4 144.4 %reduce-scatter.11.cloned.1.call-start = ((), (), s32[]{:S(2)}) async-start(), calls=%async_computation.8 | async-start | bytes 655360 | tf_op jit(solution)/shard_map/reduce_scatter | solution.py:48
  204.9 16.1 %collective-permute-start.5 = (f32[64,2048]{1,0:T(8,128)S(1)}, f32[64,2048]{1,0:T(8,128)S(1)}, u32[]{:S(2)}, u32[]{:S(2)}) collective-permute-start(f32[64,2048]{1,0:T(8,128)S(1)} %all_gather.20), channel_id=1, source_target_pairs={{4,0},{8,4},{12,8},{16,12},{20,16},{24,20},{28,24},{5,1},{9,5},{13... | collective-permute-start | bytes 1572872 | tf_op jit(solution)/shard_map/ppermute | solution.py:18
  206.2 25.9 %collective-permute-start.4 = (f32[64,2048]{1,0:T(8,128)S(1)}, f32[64,2048]{1,0:T(8,128)S(1)}, u32[]{:S(2)}, u32[]{:S(2)}) collective-permute-start(f32[64,2048]{1,0:T(8,128)S(1)} %all_gather.20), channel_id=1, source_target_pairs={{0,4},{4,8},{8,12},{12,16},{16,20},{20,24},{24,28},{1,5},{5,9},{9,... | collective-permute-start | bytes 1572872 | tf_op jit(solution)/shard_map/ppermute | solution.py:15
  242.7 89.1 %reduce-scatter.13.cloned.1.call-start = ((), (), s32[]{:S(2)}) async-start(), calls=%async_computation.9 | async-start | bytes 655360 | tf_op jit(solution)/shard_map/reduce_scatter | solution.py:48
  271.8 16.1 %collective-permute-start.7 = (f32[64,2048]{1,0:T(8,128)S(1)}, f32[64,2048]{1,0:T(8,128)S(1)}, u32[]{:S(2)}, u32[]{:S(2)}) collective-permute-start(f32[64,2048]{1,0:T(8,128)S(1)} %all_gather.21), channel_id=1, source_target_pairs={{4,0},{8,4},{12,8},{16,12},{20,16},{24,20},{28,24},{5,1},{9,5},{13... | collective-permute-start | bytes 1572872 | tf_op jit(solution)/shard_map/ppermute | solution.py:18
  273.1 25.9 %collective-permute-start.6 = (f32[64,2048]{1,0:T(8,128)S(1)}, f32[64,2048]{1,0:T(8,128)S(1)}, u32[]{:S(2)}, u32[]{:S(2)}) collective-permute-start(f32[64,2048]{1,0:T(8,128)S(1)} %all_gather.21), channel_id=1, source_target_pairs={{0,4},{4,8},{8,12},{12,16},{16,20},{20,24},{24,28},{1,5},{5,9},{9,... | collective-permute-start | bytes 1572872 | tf_op jit(solution)/shard_map/ppermute | solution.py:15
  309.5 144.4 %reduce-scatter.15.cloned.1.call-start = ((), (), s32[]{:S(2)}) async-start(), calls=%async_computation.10 | async-start | bytes 655360 | tf_op jit(solution)/shard_map/reduce_scatter | solution.py:48
  394.1 16.1 %collective-permute-start.9 = (f32[64,2048]{1,0:T(8,128)S(1)}, f32[64,2048]{1,0:T(8,128)S(1)}, u32[]{:S(2)}, u32[]{:S(2)}) collective-permute-start(f32[64,2048]{1,0:T(8,128)S(1)} %all_gather.22), channel_id=1, source_target_pairs={{4,0},{8,4},{12,8},{16,12},{20,16},{24,20},{28,24},{5,1},{9,5},{13... | collective-permute-start | bytes 1572872 | tf_op jit(solution)/shard_map/ppermute | solution.py:18
  395.4 26.0 %collective-permute-start.8 = (f32[64,2048]{1,0:T(8,128)S(1)}, f32[64,2048]{1,0:T(8,128)S(1)}, u32[]{:S(2)}, u32[]{:S(2)}) collective-permute-start(f32[64,2048]{1,0:T(8,128)S(1)} %all_gather.22), channel_id=1, source_target_pairs={{0,4},{4,8},{8,12},{12,16},{16,20},{20,24},{24,28},{1,5},{5,9},{9,... | collective-permute-start | bytes 1572872 | tf_op jit(solution)/shard_map/ppermute | solution.py:15
  431.9 89.0 %reduce-scatter.17.cloned.1.call-start = ((), (), s32[]{:S(2)}) async-start(), calls=%async_computation.11 | async-start | bytes 655360 | tf_op jit(solution)/shard_map/reduce_scatter | solution.py:48
  460.9 16.1 %collective-permute-start.11 = (f32[64,2048]{1,0:T(8,128)S(1)}, f32[64,2048]{1,0:T(8,128)S(1)}, u32[]{:S(2)}, u32[]{:S(2)}) collective-permute-start(f32[64,2048]{1,0:T(8,128)S(1)} %all_gather.23), channel_id=1, source_target_pairs={{4,0},{8,4},{12,8},{16,12},{20,16},{24,20},{28,24},{5,1},{9,5},{13... | collective-permute-start | bytes 1572872 | tf_op jit(solution)/shard_map/ppermute | solution.py:18
  462.2 25.9 %collective-permute-start.10 = (f32[64,2048]{1,0:T(8,128)S(1)}, f32[64,2048]{1,0:T(8,128)S(1)}, u32[]{:S(2)}, u32[]{:S(2)}) collective-permute-start(f32[64,2048]{1,0:T(8,128)S(1)} %all_gather.23), channel_id=1, source_target_pairs={{0,4},{4,8},{8,12},{12,16},{16,20},{20,24},{24,28},{1,5},{5,9},{9,... | collective-permute-start | bytes 1572872 | tf_op jit(solution)/shard_map/ppermute | solution.py:15
Sparse Core Ops, SparseCore 0:
  53.2 22.4 reduce-scatter.6
  120.5 22.0 reduce-scatter.8
  242.8 21.9 reduce-scatter.10
  309.6 22.0 reduce-scatter.12
  432.0 21.9 reduce-scatter.14
  498.7 22.0 reduce-scatter.16
where the time goes:
time: 584 us; the launch traced here: 583 us
  waiting for transfers between devices  260 us (45%)
  blocking collectives  165 us (28%)
  matrix products  52.7 us (9%)
  other arithmetic  38.8 us (7%)
  starting transfers between devices  35.4 us (6%)
  local copies, waits for them, and re-layouts  17.7 us (3%)
  between operations  13.8 us (2%)
    reduce_scatter x6, waiting for transfers between devices, reduce_share(): lax.psum_scatter(partial_terms, 'cols', scatter_dimension=1, tiled=True)  133 us
    psum x3, blocking collectives, per_device(): lower_factor = jnp.linalg.cholesky(lax.psum(local_gram, ('rows', 'cols')))  119 us
    ppermute x6, waiting for transfers between devices, with_halo(): lax.ppermute(lax.slice_in_dim(block, block.shape[dim] - width, None, axis...  66.9 us
    ppermute x6, waiting for transfers between devices, with_halo(): lax.ppermute(lax.slice_in_dim(block, 0, width, axis=dim), axis, backward)  59.4 us
    all_gather x6, blocking collectives, fetch_owner(): return lax.all_gather(panel_part, 'cols', axis=1, tiled=True)  45.6 us
    dot_general x6, matrix products, local_product(): jnp.einsum('disk,isnk->din', picked, tile_values, precision=lax.Precision...  44.6 us
    ppermute x6, starting transfers between devices, with_halo(): lax.ppermute(lax.slice_in_dim(block, block.shape[dim] - width, None, axis...  27.5 us
    another operation x9, other arithmetic, per_device(): lower_factor = jnp.linalg.cholesky(lax.psum(local_gram, ('rows', 'cols')))  19.6 us
  transfers between devices with their start and end apart: 18, of which 18 were waited for; matrix products, arithmetic and copies ran while one was open for 0% of the time, Pallas kernels for 0%

commit v1 on v0

--- a/solution.py
+++ b/solution.py
@@ -5,6 +5,22 @@
 from jax.sharding import PartitionSpec as P
 
 ITERS = 3
+
+
+def gather_around(x, axis, dim):
+    ways, here, step = (lax.axis_size(axis), lax.axis_index(axis), x.shape[dim])
+    shape = [n * ways if d == dim else n for d, n in enumerate(x.shape)]
+    full = lax.dynamic_update_slice_in_dim(jnp.zeros(shape, x.dtype), x, here * step, axis=dim)
+    going_up = going_down = x
+    for far in range(1, ways // 2 + 1):
+        going_up = lax.ppermute(going_up, axis, [(d, (d + 1) % ways) for d in range(ways)])
+        full = lax.dynamic_update_slice_in_dim(full, going_up, (here - far) % ways * step, axis=dim)
+        if 2 * far < ways:
+            going_down = lax.ppermute(going_down, axis, [(d, (d - 1) % ways) for d in range(ways)])
+            full = lax.dynamic_update_slice_in_dim(
+                full, going_down, (here + far) % ways * step, axis=dim
+            )
+    return full
 
 
 def with_halo(block, sides, width):
@@ -38,7 +54,7 @@
 def per_device(start_panel, tile_values, tile_column, tile_count):
 
     def fetch_owner(panel_part):
-        return lax.all_gather(panel_part, "cols", axis=1, tiled=True)
+        return gather_around(panel_part, "cols", 1)
 
     def partial_of(owner_panel):
         extended = with_halo(owner_panel, (("rows", 1),), owner_panel.shape[1])

time: 584 us -> 596 us (1.021); the launches traced: 583 us -> 588 us
  blocking collectives: 165 us -> 119 us
  waiting for transfers between devices: 260 us -> 296 us
  starting transfers between devices: 35.4 us -> 45.2 us
    ppermute x6, waiting for transfers between devices: 59.4 us -> 0.02 us  [with_halo(): lax.ppermute(lax.slice_in_dim(block, 0, width, axis=dim), axis, backward)]
    ppermute x6, waiting for transfers between devices: 66.9 us -> 118 us  [with_halo(): lax.ppermute(lax.slice_in_dim(block, block.shape[dim] - width, None, axis...]
    all_gather x6 -> x0, blocking collectives: 45.6 us -> none  [fetch_owner(): return lax.all_gather(panel_part, 'cols', axis=1, tiled=True)]
    ppermute x0 -> x18, waiting for transfers between devices: none -> 37.4 us  [the longest x12 37.4 us: gather_around(): lax.ppermute(going_up, axis, [(d, (d + 1) % ways) for d in range(ways)])]
    ppermute x0 -> x18, starting transfers between devices: none -> 15.1 us  [the longest x6 10.6 us: gather_around(): lax.ppermute(going_down, axis, [(d, (d - 1) % ways) for d in range(ways)])]
    reduce_scatter x6, waiting for transfers between devices: 133 us -> 141 us  [reduce_share(): lax.psum_scatter(partial_terms, 'cols', scatter_dimension=1, tiled=True)]
  transfers between devices with their start and end apart: 18 -> 36, of which waited for: 18 -> 24; matrix products, arithmetic and copies ran while one was open for 0% -> 1% of each run, Pallas kernels for 0% -> 0%
where the time goes in v1:
time: 596 us; the launch traced here: 588 us
  waiting for transfers between devices  296 us (50%)
  blocking collectives  119 us (20%)
  matrix products  52.7 us (9%)
  starting transfers between devices  45.2 us (8%)
  other arithmetic  38.8 us (7%)
  local copies, waits for them, and re-layouts  22 us (4%)
  between operations  14.3 us (2%)
    reduce_scatter x6, waiting for transfers between devices, reduce_share(): lax.psum_scatter(partial_terms, 'cols', scatter_dimension=1, tiled=True)  141 us
    psum x3, blocking collectives, per_device(): lower_factor = jnp.linalg.cholesky(lax.psum(local_gram, ('rows', 'cols')))  119 us
    ppermute x6, waiting for transfers between devices, with_halo(): lax.ppermute(lax.slice_in_dim(block, block.shape[dim] - width, None, axis...  118 us
    dot_general x6, matrix products, local_product(): jnp.einsum('disk,isnk->din', picked, tile_values, precision=lax.Precision...  44.6 us
    ppermute x12, waiting for transfers between devices, gather_around(): lax.ppermute(going_up, axis, [(d, (d + 1) % ways) for d in range(ways)])  37.4 us
    ppermute x6, starting transfers between devices, with_halo(): lax.ppermute(lax.slice_in_dim(block, block.shape[dim] - width, None, axis...  22.2 us
    another operation x9, other arithmetic, per_device(): lower_factor = jnp.linalg.cholesky(lax.psum(local_gram, ('rows', 'cols')))  19.6 us
    another operation x6, other arithmetic, per_device(): lax.linalg.triangular_solve(lower_factor, second, left_side=True, lower=T...  16.6 us
  transfers between devices with their start and end apart: 36, of which 24 were waited for; matrix products, arithmetic and copies ran while one was open for 1% of the time, Pallas kernels for 0%

profile of v1, /device:TPU:0, one launch (start us, length us, event | category | flops | bytes accessed | tf_op | source)
XLA Modules:
  0.0 588.3 jit_solution(4582196962419734332)
XLA Ops:
  23.5 19.3 %collective-permute-done.3 = f32[64,2048]{1,0:T(8,128)S(1)} collective-permute-done((f32[64,2048]{1,0:T(8,128)S(1)}, f32[64,2048]{1,0:T(8,128)S(1)}, u32[]{:S(2)}, u32[]{:S(2)}) %collective-permute-start.3) | collective-permute-done | bytes 524320 | tf_op jit(solution)/shard_map/ppermute | solution.py:31
  45.0 7.4 %fusion.12 = f32[16,8,8,128]{3,2,1,0:T(8,128)S(1)} fusion(f32[16,4,128,128]{3,2,1,0:T(8,128)} %param.10, f32[16,4,64,128]{3,2,1,0:T(8,128)} %bitcast.167, pred[16,4]{1,0:T(8,128)(4,1)S(1)} %copy.47, pred[16,4]{1,0:T(8,128)(4,1)S(1)} %broadcast_compare_fusion), kind=kOutput, calls=%fused_computation.36 | convolution fusion | flops 806354944 | bytes 6815872 | tf_op jit(solution)/shard_map/disk,isnk->din/dot_general | solution.py:50
  53.3 23.0 %reduce-scatter.7.cloned.1.call-done = f32[64,512]{1,0:T(8,128)} async-done(((f32[64,2048]{1,0:T(8,128)}), f32[64,512]{1,0:T(8,128)}) %reduce-scatter.7.cloned.1.call-update) | async-done | bytes 131088 | tf_op jit(solution)/shard_map/reduce_scatter | solution.py:64
  90.6 18.9 %collective-permute-done.8 = f32[64,2048]{1,0:T(8,128)S(1)} collective-permute-done((f32[64,2048]{1,0:T(8,128)S(1)}, f32[64,2048]{1,0:T(8,128)S(1)}, u32[]{:S(2)}, u32[]{:S(2)}) %collective-permute-start.8) | collective-permute-done | bytes 524320 | tf_op jit(solution)/shard_map/ppermute | solution.py:31
  111.8 7.4 %fusion.13 = f32[16,8,8,128]{3,2,1,0:T(8,128)S(1)} fusion(f32[16,4,128,128]{3,2,1,0:T(8,128)} %param.10, f32[16,4,64,128]{3,2,1,0:T(8,128)} %bitcast.168, pred[16,4]{1,0:T(8,128)(4,1)S(1)} %copy.47, pred[16,4]{1,0:T(8,128)(4,1)S(1)} %broadcast_compare_fusion), kind=kOutput, calls=%fused_computation.37 | convolution fusion | flops 806354944 | bytes 6815872 | tf_op jit(solution)/shard_map/disk,isnk->din/dot_general | solution.py:50
  120.1 24.2 %reduce-scatter.9.cloned.1.call-done = f32[64,512]{1,0:T(8,128)} async-done(((f32[64,2048]{1,0:T(8,128)}), f32[64,512]{1,0:T(8,128)}) %reduce-scatter.9.cloned.1.call-update) | async-done | bytes 131088 | tf_op jit(solution)/shard_map/reduce_scatter | solution.py:64
  145.6 40.0 %psum.21 = f32[64,64]{0,1:T(8,128)S(1)} all-reduce(f32[64,64]{0,1:T(8,128)S(1)} %fusion.69), channel_id=1, replica_groups=mesh['rows'=8,'cols'=4] {'rows','cols'}, use_global_device_ids=true, to_apply=%region_2.4 | all-reduce | flops 4096 | bytes 32768 | tf_op jit(solution)/shard_map/psum | solution.py:74
  185.7 5.8 cholesky.59
  213.4 21.0 %collective-permute-done.13 = f32[64,2048]{1,0:T(8,128)S(1)} collective-permute-done((f32[64,2048]{1,0:T(8,128)S(1)}, f32[64,2048]{1,0:T(8,128)S(1)}, u32[]{:S(2)}, u32[]{:S(2)}) %collective-permute-start.13) | collective-permute-done | bytes 524320 | tf_op jit(solution)/shard_map/ppermute | solution.py:31
  236.7 7.4 %fusion.14 = f32[16,8,8,128]{3,2,1,0:T(8,128)S(1)} fusion(f32[16,4,128,128]{3,2,1,0:T(8,128)} %param.10, f32[16,4,64,128]{3,2,1,0:T(8,128)} %bitcast.169, pred[16,4]{1,0:T(8,128)(4,1)S(1)} %copy.47, pred[16,4]{1,0:T(8,128)(4,1)S(1)} %broadcast_compare_fusion), kind=kOutput, calls=%fused_computation.38 | convolution fusion | flops 806354944 | bytes 6815872 | tf_op jit(solution)/shard_map/disk,isnk->din/dot_general | solution.py:50
  245.0 22.4 %reduce-scatter.11.cloned.1.call-done = f32[64,512]{1,0:T(8,128)} async-done(((f32[64,2048]{1,0:T(8,128)}), f32[64,512]{1,0:T(8,128)}) %reduce-scatter.11.cloned.1.call-update) | async-done | bytes 131088 | tf_op jit(solution)/shard_map/reduce_scatter | solution.py:64
  281.7 18.8 %collective-permute-done.18 = f32[64,2048]{1,0:T(8,128)S(1)} collective-permute-done((f32[64,2048]{1,0:T(8,128)S(1)}, f32[64,2048]{1,0:T(8,128)S(1)}, u32[]{:S(2)}, u32[]{:S(2)}) %collective-permute-start.18) | collective-permute-done | bytes 524320 | tf_op jit(solution)/shard_map/ppermute | solution.py:31
  302.8 7.4 %fusion.15 = f32[16,8,8,128]{3,2,1,0:T(8,128)S(1)} fusion(f32[16,4,128,128]{3,2,1,0:T(8,128)} %param.10, f32[16,4,64,128]{3,2,1,0:T(8,128)} %bitcast.170, pred[16,4]{1,0:T(8,128)(4,1)S(1)} %copy.47, pred[16,4]{1,0:T(8,128)(4,1)S(1)} %broadcast_compare_fusion), kind=kOutput, calls=%fused_computation.39 | convolution fusion | flops 806354944 | bytes 6815872 | tf_op jit(solution)/shard_map/disk,isnk->din/dot_general | solution.py:50
  311.1 24.2 %reduce-scatter.13.cloned.1.call-done = f32[64,512]{1,0:T(8,128)} async-done(((f32[64,2048]{1,0:T(8,128)}), f32[64,512]{1,0:T(8,128)}) %reduce-scatter.13.cloned.1.call-update) | async-done | bytes 131088 | tf_op jit(solution)/shard_map/reduce_scatter | solution.py:64
  336.6 39.7 %psum.22 = f32[64,64]{0,1:T(8,128)S(1)} all-reduce(f32[64,64]{0,1:T(8,128)S(1)} %fusion.70), channel_id=1, replica_groups=mesh['rows'=8,'cols'=4] {'rows','cols'}, use_global_device_ids=true, to_apply=%region_7.11 | all-reduce | flops 4096 | bytes 32768 | tf_op jit(solution)/shard_map/psum | solution.py:74
  376.4 5.8 cholesky.70
  404.2 21.0 %collective-permute-done.23 = f32[64,2048]{1,0:T(8,128)S(1)} collective-permute-done((f32[64,2048]{1,0:T(8,128)S(1)}, f32[64,2048]{1,0:T(8,128)S(1)}, u32[]{:S(2)}, u32[]{:S(2)}) %collective-permute-start.23) | collective-permute-done | bytes 524320 | tf_op jit(solution)/shard_map/ppermute | solution.py:31
  427.4 7.4 %fusion.16 = f32[16,8,8,128]{3,2,1,0:T(8,128)S(1)} fusion(f32[16,4,128,128]{3,2,1,0:T(8,128)} %param.10, f32[16,4,64,128]{3,2,1,0:T(8,128)} %bitcast.171, pred[16,4]{1,0:T(8,128)(4,1)S(1)} %copy.47, pred[16,4]{1,0:T(8,128)(4,1)S(1)} %broadcast_compare_fusion), kind=kOutput, calls=%fused_computation.40 | convolution fusion | flops 806354944 | bytes 6815872 | tf_op jit(solution)/shard_map/disk,isnk->din/dot_general | solution.py:50
  435.8 22.4 %reduce-scatter.15.cloned.1.call-done = f32[64,512]{1,0:T(8,128)} async-done(((f32[64,2048]{1,0:T(8,128)}), f32[64,512]{1,0:T(8,128)}) %reduce-scatter.15.cloned.1.call-update) | async-done | bytes 131088 | tf_op jit(solution)/shard_map/reduce_scatter | solution.py:64
  472.5 18.9 %collective-permute-done.28 = f32[64,2048]{1,0:T(8,128)S(1)} collective-permute-done((f32[64,2048]{1,0:T(8,128)S(1)}, f32[64,2048]{1,0:T(8,128)S(1)}, u32[]{:S(2)}, u32[]{:S(2)}) %collective-permute-start.28) | collective-permute-done | bytes 524320 | tf_op jit(solution)/shard_map/ppermute | solution.py:31
  493.6 7.4 %fusion.17 = f32[16,8,8,128]{3,2,1,0:T(8,128)S(1)} fusion(f32[16,4,128,128]{3,2,1,0:T(8,128)} %param.10, f32[16,4,64,128]{3,2,1,0:T(8,128)} %bitcast.166, pred[16,4]{1,0:T(8,128)(4,1)S(1)} %copy.47, pred[16,4]{1,0:T(8,128)(4,1)S(1)} %broadcast_compare_fusion), kind=kOutput, calls=%fused_computation.41 | convolution fusion | flops 806354944 | bytes 6815872 | tf_op jit(solution)/shard_map/disk,isnk->din/dot_general | solution.py:50
  501.9 24.3 %reduce-scatter.17.cloned.1.call-done = f32[64,512]{1,0:T(8,128)} async-done(((f32[64,2048]{1,0:T(8,128)}), f32[64,512]{1,0:T(8,128)}) %reduce-scatter.17.cloned.1.call-update) | async-done | bytes 131088 | tf_op jit(solution)/shard_map/reduce_scatter | solution.py:64
  527.4 39.7 %psum.23 = f32[64,64]{0,1:T(8,128)S(1)} all-reduce(f32[64,64]{0,1:T(8,128)S(1)} %fusion.71), channel_id=1, replica_groups=mesh['rows'=8,'cols'=4] {'rows','cols'}, use_global_device_ids=true, to_apply=%region_10.14 | all-reduce | flops 4096 | bytes 32768 | tf_op jit(solution)/shard_map/psum | solution.py:74
  567.2 5.8 cholesky.81
  (143 shorter events, 134.1 us)
Async XLA Ops:
  6.5 69.8 %reduce-scatter.7.cloned.1.call-start = ((), (), s32[]{:S(2)}) async-start(), calls=%async_computation.6 | async-start | bytes 655360 | tf_op jit(solution)/shard_map/reduce_scatter | solution.py:64
  7.0 6.2 %collective-permute-start.1 = (f32[64,512]{1,0:T(8,128)}, f32[64,512]{1,0:T(8,128)S(1)}, u32[]{:S(2)}, u32[]{:S(2)}) collective-permute-start(f32[64,512]{1,0:T(8,128)} %param.9), channel_id=1, source_target_pairs={{0,3},{1,0},{2,1},{3,2},{4,7},{5,4},{6,5},{7,6},{8,11},{9,8},{10,9... | collective-permute-start | bytes 393224 | tf_op jit(solution)/shard_map/ppermute | solution.py:19
  16.2 26.6 %collective-permute-start.3 = (f32[64,2048]{1,0:T(8,128)S(1)}, f32[64,2048]{1,0:T(8,128)S(1)}, u32[]{:S(2)}, u32[]{:S(2)}) collective-permute-start(f32[64,2048]{1,0:T(8,128)S(1)} %constant_dynamic-update-slice_fusion.20), channel_id=1, source_target_pairs={{0,4},{4,8},{8,12},{12,16},{16,20},{20,24},{24,28},{1,5},{5,9},{9,... | collective-permute-start | bytes 1572872 | tf_op jit(solution)/shard_map/ppermute | solution.py:31
  20.5 22.3 %collective-permute-start.4 = (f32[64,2048]{1,0:T(8,128)S(1)}, f32[64,2048]{1,0:T(8,128)S(1)}, u32[]{:S(2)}, u32[]{:S(2)}) collective-permute-start(f32[64,2048]{1,0:T(8,128)S(1)} %constant_dynamic-update-slice_fusion.20), channel_id=1, source_target_pairs={{4,0},{8,4},{12,8},{16,12},{20,16},{24,20},{28,24},{5,1},{9,5},{13... | collective-permute-start | bytes 1572872 | tf_op jit(solution)/shard_map/ppermute | solution.py:34
  53.3 91.1 %reduce-scatter.9.cloned.1.call-start = ((), (), s32[]{:S(2)}) async-start(), calls=%async_computation.7 | async-start | bytes 655360 | tf_op jit(solution)/shard_map/reduce_scatter | solution.py:64
  76.3 5.5 collective-permute-start.6
  86.2 23.3 %collective-permute-start.8 = (f32[64,2048]{1,0:T(8,128)S(1)}, f32[64,2048]{1,0:T(8,128)S(1)}, u32[]{:S(2)}, u32[]{:S(2)}) collective-permute-start(f32[64,2048]{1,0:T(8,128)S(1)} %constant_dynamic-update-slice_fusion.16), channel_id=1, source_target_pairs={{0,4},{4,8},{8,12},{12,16},{16,20},{20,24},{24,28},{1,5},{5,9},{9,... | collective-permute-start | bytes 1572872 | tf_op jit(solution)/shard_map/ppermute | solution.py:31
  89.3 20.2 %collective-permute-start.9 = (f32[64,2048]{1,0:T(8,128)S(1)}, f32[64,2048]{1,0:T(8,128)S(1)}, u32[]{:S(2)}, u32[]{:S(2)}) collective-permute-start(f32[64,2048]{1,0:T(8,128)S(1)} %constant_dynamic-update-slice_fusion.16), channel_id=1, source_target_pairs={{4,0},{8,4},{12,8},{16,12},{20,16},{24,20},{28,24},{5,1},{9,5},{13... | collective-permute-start | bytes 1572872 | tf_op jit(solution)/shard_map/ppermute | solution.py:34
  120.1 147.3 %reduce-scatter.11.cloned.1.call-start = ((), (), s32[]{:S(2)}) async-start(), calls=%async_computation.8 | async-start | bytes 655360 | tf_op jit(solution)/shard_map/reduce_scatter | solution.py:64
  199.1 5.6 collective-permute-start.11
  207.9 26.5 %collective-permute-start.13 = (f32[64,2048]{1,0:T(8,128)S(1)}, f32[64,2048]{1,0:T(8,128)S(1)}, u32[]{:S(2)}, u32[]{:S(2)}) collective-permute-start(f32[64,2048]{1,0:T(8,128)S(1)} %constant_dynamic-update-slice_fusion.12), channel_id=1, source_target_pairs={{0,4},{4,8},{8,12},{12,16},{16,20},{20,24},{24,28},{1,5},{5,9},{9,... | collective-permute-start | bytes 1572872 | tf_op jit(solution)/shard_map/ppermute | solution.py:31
  212.1 22.3 %collective-permute-start.14 = (f32[64,2048]{1,0:T(8,128)S(1)}, f32[64,2048]{1,0:T(8,128)S(1)}, u32[]{:S(2)}, u32[]{:S(2)}) collective-permute-start(f32[64,2048]{1,0:T(8,128)S(1)} %constant_dynamic-update-slice_fusion.12), channel_id=1, source_target_pairs={{4,0},{8,4},{12,8},{16,12},{20,16},{24,20},{28,24},{5,1},{9,5},{13... | collective-permute-start | bytes 1572872 | tf_op jit(solution)/shard_map/ppermute | solution.py:34
  245.0 90.4 %reduce-scatter.13.cloned.1.call-start = ((), (), s32[]{:S(2)}) async-start(), calls=%async_computation.9 | async-start | bytes 655360 | tf_op jit(solution)/shard_map/reduce_scatter | solution.py:64
  267.4 5.5 collective-permute-start.16
  277.2 23.3 %collective-permute-start.18 = (f32[64,2048]{1,0:T(8,128)S(1)}, f32[64,2048]{1,0:T(8,128)S(1)}, u32[]{:S(2)}, u32[]{:S(2)}) collective-permute-start(f32[64,2048]{1,0:T(8,128)S(1)} %constant_dynamic-update-slice_fusion.8), channel_id=1, source_target_pairs={{0,4},{4,8},{8,12},{12,16},{16,20},{20,24},{24,28},{1,5},{5,9},{9,... | collective-permute-start | bytes 1572872 | tf_op jit(solution)/shard_map/ppermute | solution.py:31
  280.4 20.2 %collective-permute-start.19 = (f32[64,2048]{1,0:T(8,128)S(1)}, f32[64,2048]{1,0:T(8,128)S(1)}, u32[]{:S(2)}, u32[]{:S(2)}) collective-permute-start(f32[64,2048]{1,0:T(8,128)S(1)} %constant_dynamic-update-slice_fusion.8), channel_id=1, source_target_pairs={{4,0},{8,4},{12,8},{16,12},{20,16},{24,20},{28,24},{5,1},{9,5},{13... | collective-permute-start | bytes 1572872 | tf_op jit(solution)/shard_map/ppermute | solution.py:34
  311.1 147.0 %reduce-scatter.15.cloned.1.call-start = ((), (), s32[]{:S(2)}) async-start(), calls=%async_computation.10 | async-start | bytes 655360 | tf_op jit(solution)/shard_map/reduce_scatter | solution.py:64
  389.9 5.6 collective-permute-start.21
  398.6 26.5 %collective-permute-start.23 = (f32[64,2048]{1,0:T(8,128)S(1)}, f32[64,2048]{1,0:T(8,128)S(1)}, u32[]{:S(2)}, u32[]{:S(2)}) collective-permute-start(f32[64,2048]{1,0:T(8,128)S(1)} %constant_dynamic-update-slice_fusion.4), channel_id=1, source_target_pairs={{0,4},{4,8},{8,12},{12,16},{16,20},{20,24},{24,28},{1,5},{5,9},{9,... | collective-permute-start | bytes 1572872 | tf_op jit(solution)/shard_map/ppermute | solution.py:31
  402.9 22.3 %collective-permute-start.24 = (f32[64,2048]{1,0:T(8,128)S(1)}, f32[64,2048]{1,0:T(8,128)S(1)}, u32[]{:S(2)}, u32[]{:S(2)}) collective-permute-start(f32[64,2048]{1,0:T(8,128)S(1)} %constant_dynamic-update-slice_fusion.4), channel_id=1, source_target_pairs={{4,0},{8,4},{12,8},{16,12},{20,16},{24,20},{28,24},{5,1},{9,5},{13... | collective-permute-start | bytes 1572872 | tf_op jit(solution)/shard_map/ppermute | solution.py:34
  435.7 90.4 %reduce-scatter.17.cloned.1.call-start = ((), (), s32[]{:S(2)}) async-start(), calls=%async_computation.11 | async-start | bytes 655360 | tf_op jit(solution)/shard_map/reduce_scatter | solution.py:64
  458.1 5.5 collective-permute-start.26
  468.0 23.3 %collective-permute-start.28 = (f32[64,2048]{1,0:T(8,128)S(1)}, f32[64,2048]{1,0:T(8,128)S(1)}, u32[]{:S(2)}, u32[]{:S(2)}) collective-permute-start(f32[64,2048]{1,0:T(8,128)S(1)} %constant_dynamic-update-slice_fusion), channel_id=1, source_target_pairs={{0,4},{4,8},{8,12},{12,16},{16,20},{20,24},{24,28},{1,5},{5,9},{9,... | collective-permute-start | bytes 1572872 | tf_op jit(solution)/shard_map/ppermute | solution.py:31
  471.2 20.2 %collective-permute-start.29 = (f32[64,2048]{1,0:T(8,128)S(1)}, f32[64,2048]{1,0:T(8,128)S(1)}, u32[]{:S(2)}, u32[]{:S(2)}) collective-permute-start(f32[64,2048]{1,0:T(8,128)S(1)} %constant_dynamic-update-slice_fusion), channel_id=1, source_target_pairs={{4,0},{8,4},{12,8},{16,12},{20,16},{24,20},{28,24},{5,1},{9,5},{13... | collective-permute-start | bytes 1572872 | tf_op jit(solution)/shard_map/ppermute | solution.py:34
  (12 other events, 56.8 us)
Sparse Core Ops, SparseCore 0:
  53.4 22.8 reduce-scatter.6
  120.2 24.1 reduce-scatter.8
  245.1 22.2 reduce-scatter.10
  311.2 24.1 reduce-scatter.12
  435.8 22.2 reduce-scatter.14
  502.0 24.1 reduce-scatter.16
